TPU v7x, 32 devices: a whole 2x2x4 slice. The times are simulated.
32 devices in a mesh: cell: 2 (over core), gene: 4 (over y, x), rank: 4 (over z).
Axes of the slice: x: 2, y: 2, z: 4, core: 2. Of those that a mesh axis runs over, the one named last changes fastest.
Arguments:
- blocks: bfloat16 [2, 16, 96, 256, 128], P('cell', ('gene', 'rank')), may hold values from -6 to 6
- block_pos: int32 [2, 16, 96], P('cell', ('gene', 'rank')), may hold values from 0 to 127, as said below
- block_count: int32 [2, 16], P('cell', ('gene', 'rank')), may hold values from 32 to 96, as said below
- test_right: bfloat16 [32768, 512], P(('gene', 'rank')), may hold values from -0.0625 to 0.0625
- test_left: bfloat16 [4096, 768], P('cell', 'rank'), may hold values from -0.1875 to 0.1875
- gene_sketch_old: float32 [768, 32768], P('cell', ('gene', 'rank')), may hold values from -4 to 4
Outputs:
- right_sketch: float32 [4096, 512], P(('cell', 'gene', 'rank'))
- gene_sketch: float32 [768, 32768], P('cell', ('gene', 'rank'))
- core: float32 [768, 512], P('cell')
Inputs may be any that keep to these rules, and one draw needn't show every extreme that they name: `block_pos`: position p names row block p // 16 and gene block p % 16 of the device's tile; the 96 positions of one device are distinct. `block_count`: some device has all 96 slots live in every draw; slots from the count on are not part of A.
All inputs are finite; a program needn't handle non-finite values.
Results may differ from a plain program's by a relative error of at most 0.0003.
Values may be sent and summed in bfloat16 or wider, within the bound.
A program may use at most 128 MiB of HBM per device.

v0:
```python
import jax
import jax.numpy as jnp
from jax import lax
from jax.sharding import PartitionSpec as P

GROUP = 16


def body(blocks, block_pos, block_count, test_right, test_left, gene_sketch_old):
    highest = lax.Precision.HIGHEST
    tiles = blocks[0, 0]
    positions = block_pos[0, 0]
    live_count = block_count[0, 0]
    slots, block_rows, block_cols = tiles.shape
    gene_blocks = test_right.shape[0] // block_cols
    right_width = test_right.shape[1]
    left_full = lax.all_gather(test_left, "rank", axis=1, tiled=True)
    row_blocks = left_full.shape[0] // block_rows
    left_width = left_full.shape[1]
    right_table = test_right.reshape(gene_blocks, block_cols, right_width)
    left_table = left_full.reshape(row_blocks, block_rows, left_width)
    offsets = jnp.arange(GROUP, dtype=jnp.int32)

    def visit(turn_index, carry):
        right_acc, gene_acc = carry
        first_slot = turn_index * GROUP
        group_tiles = lax.dynamic_slice_in_dim(tiles, first_slot, GROUP, 0)
        group_places = lax.dynamic_slice_in_dim(positions, first_slot, GROUP, 0)
        alive_mask = (first_slot + offsets < live_count).astype(jnp.float32)
        row_block = group_places // gene_blocks
        gene_block = group_places % gene_blocks
        right_rows = jnp.take(right_table, gene_block, axis=0)
        left_rows = jnp.take(left_table, row_block, axis=0)
        right_terms = (
            jnp.einsum("pik,pkr->pir", group_tiles, right_rows, preferred_element_type=jnp.float32)
            * alive_mask[:, None, None]
        )
        gene_terms = (
            jnp.einsum("pil,pik->lpk", left_rows, group_tiles, preferred_element_type=jnp.float32)
            * alive_mask[None, :, None]
        )
        right_acc = right_acc.at[row_block].add(right_terms)
        gene_acc = gene_acc.at[:, gene_block].add(gene_terms)
        return (right_acc, gene_acc)

    turn_count = (live_count + GROUP - 1) // GROUP
    initial = (
        jnp.zeros((row_blocks, block_rows, right_width), jnp.float32),
        jnp.zeros((left_width, gene_blocks, block_cols), jnp.float32),
    )
    right_part, gene_part = lax.fori_loop(0, turn_count, visit, initial)
    right_flat = right_part.reshape(row_blocks * block_rows, right_width)
    gene_flat = gene_part.reshape(left_width, gene_blocks * block_cols)
    right_half = lax.psum_scatter(right_flat, "gene", scatter_dimension=0, tiled=True)
    right_mine = lax.psum_scatter(right_half, "rank", scatter_dimension=0, tiled=True)
    gene_mine = lax.psum_scatter(gene_flat, "cell", scatter_dimension=0, tiled=True)
    gene_sketch = gene_sketch_old + gene_mine
    shard_index = lax.axis_index("gene") * lax.axis_size("rank") + lax.axis_index("rank")
    mine_rows = right_mine.shape[0]
    left_mine = lax.dynamic_slice_in_dim(left_full, shard_index * mine_rows, mine_rows, 0).astype(
        jnp.float32
    )
    core_part = lax.dot_general(left_mine, right_mine, (((0,), (0,)), ((), ())), precision=highest)
    core_total = lax.psum(core_part, ("cell", "gene", "rank"))
    share = left_width // lax.axis_size("cell")
    core = lax.dynamic_slice_in_dim(core_total, lax.axis_index("cell") * share, share, 0)
    return (right_mine, gene_sketch, core)


def solution(mesh):
    return jax.shard_map(
        body,
        mesh=mesh,
        in_specs=(
            P("cell", ("gene", "rank"), None, None, None),
            P("cell", ("gene", "rank"), None),
            P("cell", ("gene", "rank")),
            P(("gene", "rank"), None),
            P("cell", "rank"),
            P("cell", ("gene", "rank")),
        ),
        out_specs=(P(("cell", "gene", "rank"), None), P("cell", ("gene", "rank")), P("cell", None)),
        check_vma=False,
    )
```

profile of v0, /device:TPU:1, one launch (start us, length us, event | category | flops | bytes accessed | tf_op | source)
XLA Modules:
  0.0 695.8 jit_solution(15199658908383752672)
XLA Ops:
  8.6 66.3 %all-gather.2.cloned.1.call-done = bf16[2048,768]{0,1:T(8,128)(2,1)} async-done(((bf16[2048,192]{0,1:T(8,128)(2,1)}), bf16[2048,768]{0,1:T(8,128)(2,1)}) %all-gather.2.cloned.1.call-update) | async-done | bytes 3145744 | tf_op jit(solution)/shard_map/all_gather | solution.py:17
  84.0 305.6 %while.15 = (s32[]{:T(128)}, f32[8,256,512]{2,1,0:T(8,128)}, f32[768,16,128]{2,0,1:T(8,128)}, s32[]{:T(128)}, s32[96]{0:T(128)S(1)}, /*index=5*/bf16[96,256,128]...) while((s32[]{:T(128)}, f32[8,256,512]{2,1,0:T(8,128)}, ...), condition=%wide.region_3.4_spmd.clone, body=%wide.region_0.3_spmd.clone.sunk | while | flops 1353714176 | bytes 98575488 | solution.py:51
  88.3 7.2 %multiply_bitcast_fusion.2 = f32[16,768,128]{1,2,0:T(8,128)} fusion(f32[16]{0:T(128)S(1)} %get-tuple-element.245, bf16[16,256,768]{2,1,0:T(8,128)(2,1)} %gather_fusion.1, pred[16]{0:T(512)(128)(4,1)S(1)} %get-tuple-element.249, bf16[96,256,128]{2,1,0:T(8,128)(2,1)} %get-tuple-element.281, s32[]{:T(128)S(6)} %select_n.101), kind=kOutput, calls=%fused_computation.5.clone.1 | convolution fusion | flops 810024960 | bytes 13631572 | tf_op jit(solution)/shard_map/while/body/pil,pik->lpk/dot_general | solution.py:39
  95.5 6.5 copy.17
  102.0 15.0 %scatter_fusion.1 = f32[768,16,128]{2,0,1:T(8,128)} fusion(f32[768,16,128]{2,0,1:T(8,128)} %get-tuple-element.265, s32[16]{0:T(128)S(1)} %get-tuple-element.247, f32[16,768,128]{2,1,0:T(8,128)} %copy.17), kind=kCustom, calls=%fused_computation.3.clone.clone.1 | custom fusion | flops 1572864 | bytes 18874432 | tf_op jit(solution)/shard_map/while/body/scatter-add | solution.py:43
  127.1 18.1 %scatter_fusion = f32[8,256,512]{2,1,0:T(8,128)} fusion(f32[8,256,512]{2,1,0:T(8,128)} %get-tuple-element.264, s32[16]{0:T(128)S(1)} %get-tuple-element.244, f32[16,256,512]{2,1,0:T(8,128)} %broadcast_multiply_fusion.2), kind=kCustom, calls=%fused_computation.2.clone.clone.1 | custom fusion | flops 2097152 | bytes 25165888 | tf_op jit(solution)/shard_map/while/body/scatter-add | solution.py:42
  149.4 7.2 %multiply_bitcast_fusion.2 = f32[16,768,128]{1,2,0:T(8,128)} fusion(f32[16]{0:T(128)S(1)} %get-tuple-element.245, bf16[16,256,768]{2,1,0:T(8,128)(2,1)} %gather_fusion.1, pred[16]{0:T(512)(128)(4,1)S(1)} %get-tuple-element.249, bf16[96,256,128]{2,1,0:T(8,128)(2,1)} %get-tuple-element.281, s32[]{:T(128)S(6)} %select_n.101), kind=kOutput, calls=%fused_computation.5.clone.1 | convolution fusion | flops 810024960 | bytes 13631572 | tf_op jit(solution)/shard_map/while/body/pil,pik->lpk/dot_general | solution.py:39
  156.6 6.5 copy.17
  163.2 15.3 %scatter_fusion.1 = f32[768,16,128]{2,0,1:T(8,128)} fusion(f32[768,16,128]{2,0,1:T(8,128)} %get-tuple-element.265, s32[16]{0:T(128)S(1)} %get-tuple-element.247, f32[16,768,128]{2,1,0:T(8,128)} %copy.17), kind=kCustom, calls=%fused_computation.3.clone.clone.1 | custom fusion | flops 1572864 | bytes 18874432 | tf_op jit(solution)/shard_map/while/body/scatter-add | solution.py:43
  188.5 18.0 %scatter_fusion = f32[8,256,512]{2,1,0:T(8,128)} fusion(f32[8,256,512]{2,1,0:T(8,128)} %get-tuple-element.264, s32[16]{0:T(128)S(1)} %get-tuple-element.244, f32[16,256,512]{2,1,0:T(8,128)} %broadcast_multiply_fusion.2), kind=kCustom, calls=%fused_computation.2.clone.clone.1 | custom fusion | flops 2097152 | bytes 25165888 | tf_op jit(solution)/shard_map/while/body/scatter-add | solution.py:42
  210.8 7.2 %multiply_bitcast_fusion.2 = f32[16,768,128]{1,2,0:T(8,128)} fusion(f32[16]{0:T(128)S(1)} %get-tuple-element.245, bf16[16,256,768]{2,1,0:T(8,128)(2,1)} %gather_fusion.1, pred[16]{0:T(512)(128)(4,1)S(1)} %get-tuple-element.249, bf16[96,256,128]{2,1,0:T(8,128)(2,1)} %get-tuple-element.281, s32[]{:T(128)S(6)} %select_n.101), kind=kOutput, calls=%fused_computation.5.clone.1 | convolution fusion | flops 810024960 | bytes 13631572 | tf_op jit(solution)/shard_map/while/body/pil,pik->lpk/dot_general | solution.py:39
  218.0 6.5 copy.17
  224.6 14.9 %scatter_fusion.1 = f32[768,16,128]{2,0,1:T(8,128)} fusion(f32[768,16,128]{2,0,1:T(8,128)} %get-tuple-element.265, s32[16]{0:T(128)S(1)} %get-tuple-element.247, f32[16,768,128]{2,1,0:T(8,128)} %copy.17), kind=kCustom, calls=%fused_computation.3.clone.clone.1 | custom fusion | flops 1572864 | bytes 18874432 | tf_op jit(solution)/shard_map/while/body/scatter-add | solution.py:43
  249.6 18.0 %scatter_fusion = f32[8,256,512]{2,1,0:T(8,128)} fusion(f32[8,256,512]{2,1,0:T(8,128)} %get-tuple-element.264, s32[16]{0:T(128)S(1)} %get-tuple-element.244, f32[16,256,512]{2,1,0:T(8,128)} %broadcast_multiply_fusion.2), kind=kCustom, calls=%fused_computation.2.clone.clone.1 | custom fusion | flops 2097152 | bytes 25165888 | tf_op jit(solution)/shard_map/while/body/scatter-add | solution.py:42
  271.9 7.2 %multiply_bitcast_fusion.2 = f32[16,768,128]{1,2,0:T(8,128)} fusion(f32[16]{0:T(128)S(1)} %get-tuple-element.245, bf16[16,256,768]{2,1,0:T(8,128)(2,1)} %gather_fusion.1, pred[16]{0:T(512)(128)(4,1)S(1)} %get-tuple-element.249, bf16[96,256,128]{2,1,0:T(8,128)(2,1)} %get-tuple-element.281, s32[]{:T(128)S(6)} %select_n.101), kind=kOutput, calls=%fused_computation.5.clone.1 | convolution fusion | flops 810024960 | bytes 13631572 | tf_op jit(solution)/shard_map/while/body/pil,pik->lpk/dot_general | solution.py:39
  285.6 15.1 %scatter_fusion.1 = f32[768,16,128]{2,0,1:T(8,128)} fusion(f32[768,16,128]{2,0,1:T(8,128)} %get-tuple-element.265, s32[16]{0:T(128)S(1)} %get-tuple-element.247, f32[16,768,128]{2,1,0:T(8,128)} %copy.17), kind=kCustom, calls=%fused_computation.3.clone.clone.1 | custom fusion | flops 1572864 | bytes 18874432 | tf_op jit(solution)/shard_map/while/body/scatter-add | solution.py:43
  310.8 17.6 %scatter_fusion = f32[8,256,512]{2,1,0:T(8,128)} fusion(f32[8,256,512]{2,1,0:T(8,128)} %get-tuple-element.264, s32[16]{0:T(128)S(1)} %get-tuple-element.244, f32[16,256,512]{2,1,0:T(8,128)} %broadcast_multiply_fusion.2), kind=kCustom, calls=%fused_computation.2.clone.clone.1 | custom fusion | flops 2097152 | bytes 25165888 | tf_op jit(solution)/shard_map/while/body/scatter-add | solution.py:42
  332.7 7.2 %multiply_bitcast_fusion.2 = f32[16,768,128]{1,2,0:T(8,128)} fusion(f32[16]{0:T(128)S(1)} %get-tuple-element.245, bf16[16,256,768]{2,1,0:T(8,128)(2,1)} %gather_fusion.1, pred[16]{0:T(512)(128)(4,1)S(1)} %get-tuple-element.249, bf16[96,256,128]{2,1,0:T(8,128)(2,1)} %get-tuple-element.281, s32[]{:T(128)S(6)} %select_n.101), kind=kOutput, calls=%fused_computation.5.clone.1 | convolution fusion | flops 810024960 | bytes 13631572 | tf_op jit(solution)/shard_map/while/body/pil,pik->lpk/dot_general | solution.py:39
  346.4 15.1 %scatter_fusion.1 = f32[768,16,128]{2,0,1:T(8,128)} fusion(f32[768,16,128]{2,0,1:T(8,128)} %get-tuple-element.265, s32[16]{0:T(128)S(1)} %get-tuple-element.247, f32[16,768,128]{2,1,0:T(8,128)} %copy.17), kind=kCustom, calls=%fused_computation.3.clone.clone.1 | custom fusion | flops 1572864 | bytes 18874432 | tf_op jit(solution)/shard_map/while/body/scatter-add | solution.py:43
  371.7 18.0 %scatter_fusion = f32[8,256,512]{2,1,0:T(8,128)} fusion(f32[8,256,512]{2,1,0:T(8,128)} %get-tuple-element.264, s32[16]{0:T(128)S(1)} %get-tuple-element.244, f32[16,256,512]{2,1,0:T(8,128)} %broadcast_multiply_fusion.2), kind=kCustom, calls=%fused_computation.2.clone.clone.1 | custom fusion | flops 2097152 | bytes 25165888 | tf_op jit(solution)/shard_map/while/body/scatter-add | solution.py:42
  389.7 112.0 %reduce-scatter.4.cloned.1.call-done = f32[512,512]{1,0:T(8,128)} async-done(((f32[2048,512]{1,0:T(8,128)}), f32[512,512]{1,0:T(8,128)}) %reduce-scatter.4.cloned.1.call-update) | async-done | bytes 1048592 | tf_op jit(solution)/shard_map/reduce_scatter | solution.py:54
  501.8 29.9 %reduce-scatter.6.cloned.1.call-done = f32[128,512]{1,0:T(8,128)} async-done(((f32[512,512]{1,0:T(8,128)}), f32[128,512]{1,0:T(8,128)}) %reduce-scatter.6.cloned.1.call-update) | async-done | bytes 262160 | tf_op jit(solution)/shard_map/reduce_scatter | solution.py:55
  541.1 126.8 %all-reduce.2.cloned.1.call-done = f32[768,512]{1,0:T(8,128)} async-done(((f32[768,512]{1,0:T(8,128)}), f32[768,512]{1,0:T(8,128)}) %all-reduce.2.cloned.1.call-update) | async-done | bytes 1572880 | tf_op jit(solution)/shard_map/psum | solution.py:64
  670.0 15.3 %reduce-scatter.8.cloned.1.call-done = f32[384,2048]{1,0:T(8,128)} async-done(((f32[768,2048]{1,0:T(8,128)}), f32[384,2048]{1,0:T(8,128)}) %reduce-scatter.8.cloned.1.call-update) | async-done | bytes 3145744 | tf_op jit(solution)/shard_map/reduce_scatter | solution.py:56
  (58 shorter events, 110.3 us)
Async XLA Ops:
  7.2 67.8 %all-gather.2.cloned.1.call-start = ((), (), s32[]{:S(2)}) async-start(), calls=%async_computation.3 | async-start | bytes 3932160 | tf_op jit(solution)/shard_map/all_gather | solution.py:17
  7.9 493.9 %reduce-scatter.4.cloned.1.call-start = ((), (), s32[]{:S(2)}) async-start(), calls=%async_computation.4 | async-start | bytes 5242880 | tf_op jit(solution)/shard_map/reduce_scatter | solution.py:54
  78.1 5.9 copy-start.1
  389.7 142.1 %reduce-scatter.6.cloned.1.call-start = ((), (), s32[]{:S(2)}) async-start(), calls=%async_computation.5 | async-start | bytes 1310720 | tf_op jit(solution)/shard_map/reduce_scatter | solution.py:55
  501.8 166.1 %all-reduce.2.cloned.1.call-start = ((), (), s32[]{:S(2)}) async-start(), calls=%async_computation.7 | async-start | bytes 3145728 | tf_op jit(solution)/shard_map/psum | solution.py:64
  534.7 150.5 %reduce-scatter.8.cloned.1.call-start = ((), (), s32[]{:S(2)}) async-start(), calls=%async_computation.6 | async-start | bytes 9437184 | tf_op jit(solution)/shard_map/reduce_scatter | solution.py:56
  541.1 144.1 %copy-start = (f32[384,2048]{1,0:T(8,128)S(1)}, f32[384,2048]{1,0:T(8,128)}, u32[]{:S(2)}) copy-start(f32[384,2048]{1,0:T(8,128)} %param.13) | copy-start | bytes 9437188
Sparse Core Ops, SparseCore 0:
  9.5 65.3 all-gather.1
  389.8 111.9 reduce-scatter.3
  504.6 27.0 reduce-scatter.5
  537.4 130.4 all-reduce.1
  670.1 15.1 reduce-scatter.7
where the time goes:
time: 697 us; the launch traced here: 696 us
  waiting for transfers between devices  351 us (50%)
  other arithmetic  173 us (25%)
  local copies, waits for them, and re-layouts  85.8 us (12%)
  matrix products  71.3 us (10%)
  between operations  14.5 us (2%)
    psum x1, waiting for transfers between devices, body(): core_total = lax.psum(core_part, ('cell', 'gene', 'rank'))  127 us
    reduce_scatter x1, waiting for transfers between devices, body(): lax.psum_scatter(right_flat, 'gene', scatter_dimension=0, tiled=True)  112 us
    scatter-add x5, other arithmetic, visit(): right_acc = right_acc.at[row_block].add(right_terms)  89.7 us
    scatter-add x5, other arithmetic, visit(): gene_acc = gene_acc.at[:, gene_block].add(gene_terms)  75.5 us
    all_gather x1, waiting for transfers between devices, body(): left_full = lax.all_gather(test_left, 'rank', axis=1, tiled=True)  66.3 us
    dot_general x5, matrix products, visit(): jnp.einsum('pil,pik->lpk', left_rows, group_tiles, preferred_element_type...  35.9 us
    mul x5, local copies, waits for them, and re-layouts, visit(): jnp.einsum('pil,pik->lpk', left_rows, group_tiles, preferred_element_type...  32.7 us
    dot_general x5, matrix products, visit(): jnp.einsum('pik,pkr->pir', group_tiles, right_rows, preferred_element_typ...  32.4 us
  transfers between devices with their start and end apart: 5, of which 5 were waited for; matrix products, arithmetic and copies ran while one was open for 1% of the time, Pallas kernels for 0%

commit v1 on v0

--- a/solution.py
+++ b/solution.py
@@ -61,7 +61,7 @@
         jnp.float32
     )
     core_part = lax.dot_general(left_mine, right_mine, (((0,), (0,)), ((), ())), precision=highest)
-    core_total = lax.psum(core_part, ("cell", "gene", "rank"))
+    core_total = lax.psum(lax.psum(core_part, "cell"), ("gene", "rank"))
     share = left_width // lax.axis_size("cell")
     core = lax.dynamic_slice_in_dim(core_total, lax.axis_index("cell") * share, share, 0)
     return (right_mine, gene_sketch, core)

time: 697 us -> 708 us (1.016)
  waiting for transfers between devices: 351 us -> 359 us
    psum x1 -> x2, waiting for transfers between devices: 127 us -> 133 us  [body(): core_total = lax.psum(lax.psum(core_part, 'cell'), ('gene', 'rank'))]
  transfers between devices with their start and end apart: 5 -> 6, of which waited for: 5 -> 6; matrix products, arithmetic and copies ran while one was open for 1% -> 1% of each run, Pallas kernels for 0% -> 0%
where the time goes in v1:
time: 708 us; the launch traced here: 705 us
  waiting for transfers between devices  359 us (51%)
  other arithmetic  173 us (24%)
  local copies, waits for them, and re-layouts  85.9 us (12%)
  matrix products  71.3 us (10%)
  between operations  14.8 us (2%)
    psum x2, waiting for transfers between devices, body(): core_total = lax.psum(lax.psum(core_part, 'cell'), ('gene', 'rank'))  133 us
    reduce_scatter x1, waiting for transfers between devices, body(): lax.psum_scatter(right_flat, 'gene', scatter_dimension=0, tiled=True)  112 us
    scatter-add x5, other arithmetic, visit(): right_acc = right_acc.at[row_block].add(right_terms)  89.7 us
    scatter-add x5, other arithmetic, visit(): gene_acc = gene_acc.at[:, gene_block].add(gene_terms)  75.5 us
    all_gather x1, waiting for transfers between devices, body(): left_full = lax.all_gather(test_left, 'rank', axis=1, tiled=True)  66.3 us
    dot_general x5, matrix products, visit(): jnp.einsum('pil,pik->lpk', left_rows, group_tiles, preferred_element_type...  35.9 us
    mul x5, local copies, waits for them, and re-layouts, visit(): jnp.einsum('pil,pik->lpk', left_rows, group_tiles, preferred_element_type...  32.7 us
    dot_general x5, matrix products, visit(): jnp.einsum('pik,pkr->pir', group_tiles, right_rows, preferred_element_typ...  32.4 us
  transfers between devices with their start and end apart: 6, of which 6 were waited for; matrix products, arithmetic and copies ran while one was open for 1% of the time, Pallas kernels for 0%

profile of v1, /device:TPU:1, one launch (start us, length us, event | category | flops | bytes accessed | tf_op | source)
XLA Modules:
  0.0 704.5 jit_solution(8445042487540783814)
XLA Ops:
  8.6 66.3 %all-gather.2.cloned.1.call-done = bf16[2048,768]{0,1:T(8,128)(2,1)} async-done(((bf16[2048,192]{0,1:T(8,128)(2,1)}), bf16[2048,768]{0,1:T(8,128)(2,1)}) %all-gather.2.cloned.1.call-update) | async-done | bytes 3145744 | tf_op jit(solution)/shard_map/all_gather | solution.py:17
  84.0 305.6 %while.15 = (s32[]{:T(128)}, f32[8,256,512]{2,1,0:T(8,128)}, f32[768,16,128]{2,0,1:T(8,128)}, s32[]{:T(128)}, s32[96]{0:T(128)S(1)}, /*index=5*/bf16[96,256,128]...) while((s32[]{:T(128)}, f32[8,256,512]{2,1,0:T(8,128)}, ...), condition=%wide.region_3.4_spmd.clone, body=%wide.region_0.3_spmd.clone.sunk | while | flops 1353714176 | bytes 98575488 | solution.py:51
  88.3 7.2 %multiply_bitcast_fusion.2 = f32[16,768,128]{1,2,0:T(8,128)} fusion(f32[16]{0:T(128)S(1)} %get-tuple-element.245, bf16[16,256,768]{2,1,0:T(8,128)(2,1)} %gather_fusion.1, pred[16]{0:T(512)(128)(4,1)S(1)} %get-tuple-element.249, bf16[96,256,128]{2,1,0:T(8,128)(2,1)} %get-tuple-element.281, s32[]{:T(128)S(6)} %select_n.101), kind=kOutput, calls=%fused_computation.5.clone.1 | convolution fusion | flops 810024960 | bytes 13631572 | tf_op jit(solution)/shard_map/while/body/pil,pik->lpk/dot_general | solution.py:39
  95.5 6.5 copy.17
  102.0 15.0 %scatter_fusion.1 = f32[768,16,128]{2,0,1:T(8,128)} fusion(f32[768,16,128]{2,0,1:T(8,128)} %get-tuple-element.265, s32[16]{0:T(128)S(1)} %get-tuple-element.247, f32[16,768,128]{2,1,0:T(8,128)} %copy.17), kind=kCustom, calls=%fused_computation.3.clone.clone.1 | custom fusion | flops 1572864 | bytes 18874432 | tf_op jit(solution)/shard_map/while/body/scatter-add | solution.py:43
  127.1 18.1 %scatter_fusion = f32[8,256,512]{2,1,0:T(8,128)} fusion(f32[8,256,512]{2,1,0:T(8,128)} %get-tuple-element.264, s32[16]{0:T(128)S(1)} %get-tuple-element.244, f32[16,256,512]{2,1,0:T(8,128)} %broadcast_multiply_fusion.2), kind=kCustom, calls=%fused_computation.2.clone.clone.1 | custom fusion | flops 2097152 | bytes 25165888 | tf_op jit(solution)/shard_map/while/body/scatter-add | solution.py:42
  149.4 7.2 %multiply_bitcast_fusion.2 = f32[16,768,128]{1,2,0:T(8,128)} fusion(f32[16]{0:T(128)S(1)} %get-tuple-element.245, bf16[16,256,768]{2,1,0:T(8,128)(2,1)} %gather_fusion.1, pred[16]{0:T(512)(128)(4,1)S(1)} %get-tuple-element.249, bf16[96,256,128]{2,1,0:T(8,128)(2,1)} %get-tuple-element.281, s32[]{:T(128)S(6)} %select_n.101), kind=kOutput, calls=%fused_computation.5.clone.1 | convolution fusion | flops 810024960 | bytes 13631572 | tf_op jit(solution)/shard_map/while/body/pil,pik->lpk/dot_general | solution.py:39
  156.6 6.5 copy.17
  163.2 15.3 %scatter_fusion.1 = f32[768,16,128]{2,0,1:T(8,128)} fusion(f32[768,16,128]{2,0,1:T(8,128)} %get-tuple-element.265, s32[16]{0:T(128)S(1)} %get-tuple-element.247, f32[16,768,128]{2,1,0:T(8,128)} %copy.17), kind=kCustom, calls=%fused_computation.3.clone.clone.1 | custom fusion | flops 1572864 | bytes 18874432 | tf_op jit(solution)/shard_map/while/body/scatter-add | solution.py:43
  188.5 18.0 %scatter_fusion = f32[8,256,512]{2,1,0:T(8,128)} fusion(f32[8,256,512]{2,1,0:T(8,128)} %get-tuple-element.264, s32[16]{0:T(128)S(1)} %get-tuple-element.244, f32[16,256,512]{2,1,0:T(8,128)} %broadcast_multiply_fusion.2), kind=kCustom, calls=%fused_computation.2.clone.clone.1 | custom fusion | flops 2097152 | bytes 25165888 | tf_op jit(solution)/shard_map/while/body/scatter-add | solution.py:42
  210.8 7.2 %multiply_bitcast_fusion.2 = f32[16,768,128]{1,2,0:T(8,128)} fusion(f32[16]{0:T(128)S(1)} %get-tuple-element.245, bf16[16,256,768]{2,1,0:T(8,128)(2,1)} %gather_fusion.1, pred[16]{0:T(512)(128)(4,1)S(1)} %get-tuple-element.249, bf16[96,256,128]{2,1,0:T(8,128)(2,1)} %get-tuple-element.281, s32[]{:T(128)S(6)} %select_n.101), kind=kOutput, calls=%fused_computation.5.clone.1 | convolution fusion | flops 810024960 | bytes 13631572 | tf_op jit(solution)/shard_map/while/body/pil,pik->lpk/dot_general | solution.py:39
  224.6 14.9 %scatter_fusion.1 = f32[768,16,128]{2,0,1:T(8,128)} fusion(f32[768,16,128]{2,0,1:T(8,128)} %get-tuple-element.265, s32[16]{0:T(128)S(1)} %get-tuple-element.247, f32[16,768,128]{2,1,0:T(8,128)} %copy.17), kind=kCustom, calls=%fused_computation.3.clone.clone.1 | custom fusion | flops 1572864 | bytes 18874432 | tf_op jit(solution)/shard_map/while/body/scatter-add | solution.py:43
  249.6 18.0 %scatter_fusion = f32[8,256,512]{2,1,0:T(8,128)} fusion(f32[8,256,512]{2,1,0:T(8,128)} %get-tuple-element.264, s32[16]{0:T(128)S(1)} %get-tuple-element.244, f32[16,256,512]{2,1,0:T(8,128)} %broadcast_multiply_fusion.2), kind=kCustom, calls=%fused_computation.2.clone.clone.1 | custom fusion | flops 2097152 | bytes 25165888 | tf_op jit(solution)/shard_map/while/body/scatter-add | solution.py:42
  271.9 7.2 %multiply_bitcast_fusion.2 = f32[16,768,128]{1,2,0:T(8,128)} fusion(f32[16]{0:T(128)S(1)} %get-tuple-element.245, bf16[16,256,768]{2,1,0:T(8,128)(2,1)} %gather_fusion.1, pred[16]{0:T(512)(128)(4,1)S(1)} %get-tuple-element.249, bf16[96,256,128]{2,1,0:T(8,128)(2,1)} %get-tuple-element.281, s32[]{:T(128)S(6)} %select_n.101), kind=kOutput, calls=%fused_computation.5.clone.1 | convolution fusion | flops 810024960 | bytes 13631572 | tf_op jit(solution)/shard_map/while/body/pil,pik->lpk/dot_general | solution.py:39
  285.6 15.1 %scatter_fusion.1 = f32[768,16,128]{2,0,1:T(8,128)} fusion(f32[768,16,128]{2,0,1:T(8,128)} %get-tuple-element.265, s32[16]{0:T(128)S(1)} %get-tuple-element.247, f32[16,768,128]{2,1,0:T(8,128)} %copy.17), kind=kCustom, calls=%fused_computation.3.clone.clone.1 | custom fusion | flops 1572864 | bytes 18874432 | tf_op jit(solution)/shard_map/while/body/scatter-add | solution.py:43
  310.8 17.6 %scatter_fusion = f32[8,256,512]{2,1,0:T(8,128)} fusion(f32[8,256,512]{2,1,0:T(8,128)} %get-tuple-element.264, s32[16]{0:T(128)S(1)} %get-tuple-element.244, f32[16,256,512]{2,1,0:T(8,128)} %broadcast_multiply_fusion.2), kind=kCustom, calls=%fused_computation.2.clone.clone.1 | custom fusion | flops 2097152 | bytes 25165888 | tf_op jit(solution)/shard_map/while/body/scatter-add | solution.py:42
  332.7 7.2 %multiply_bitcast_fusion.2 = f32[16,768,128]{1,2,0:T(8,128)} fusion(f32[16]{0:T(128)S(1)} %get-tuple-element.245, bf16[16,256,768]{2,1,0:T(8,128)(2,1)} %gather_fusion.1, pred[16]{0:T(512)(128)(4,1)S(1)} %get-tuple-element.249, bf16[96,256,128]{2,1,0:T(8,128)(2,1)} %get-tuple-element.281, s32[]{:T(128)S(6)} %select_n.101), kind=kOutput, calls=%fused_computation.5.clone.1 | convolution fusion | flops 810024960 | bytes 13631572 | tf_op jit(solution)/shard_map/while/body/pil,pik->lpk/dot_general | solution.py:39
  346.4 15.1 %scatter_fusion.1 = f32[768,16,128]{2,0,1:T(8,128)} fusion(f32[768,16,128]{2,0,1:T(8,128)} %get-tuple-element.265, s32[16]{0:T(128)S(1)} %get-tuple-element.247, f32[16,768,128]{2,1,0:T(8,128)} %copy.17), kind=kCustom, calls=%fused_computation.3.clone.clone.1 | custom fusion | flops 1572864 | bytes 18874432 | tf_op jit(solution)/shard_map/while/body/scatter-add | solution.py:43
  371.7 18.0 %scatter_fusion = f32[8,256,512]{2,1,0:T(8,128)} fusion(f32[8,256,512]{2,1,0:T(8,128)} %get-tuple-element.264, s32[16]{0:T(128)S(1)} %get-tuple-element.244, f32[16,256,512]{2,1,0:T(8,128)} %broadcast_multiply_fusion.2), kind=kCustom, calls=%fused_computation.2.clone.clone.1 | custom fusion | flops 2097152 | bytes 25165888 | tf_op jit(solution)/shard_map/while/body/scatter-add | solution.py:42
  389.7 112.0 %reduce-scatter.4.cloned.1.call-done = f32[512,512]{1,0:T(8,128)} async-done(((f32[2048,512]{1,0:T(8,128)}), f32[512,512]{1,0:T(8,128)}) %reduce-scatter.4.cloned.1.call-update) | async-done | bytes 1048592 | tf_op jit(solution)/shard_map/reduce_scatter | solution.py:54
  501.8 29.9 %reduce-scatter.6.cloned.1.call-done = f32[128,512]{1,0:T(8,128)} async-done(((f32[512,512]{1,0:T(8,128)}), f32[128,512]{1,0:T(8,128)}) %reduce-scatter.6.cloned.1.call-update) | async-done | bytes 262160 | tf_op jit(solution)/shard_map/reduce_scatter | solution.py:55
  541.2 13.3 %all-reduce.3.cloned.1.call-done = f32[768,512]{1,0:T(8,128)} async-done(((f32[768,512]{1,0:T(8,128)}), f32[768,512]{1,0:T(8,128)}) %all-reduce.3.cloned.1.call-update) | async-done | bytes 1572880 | tf_op jit(solution)/shard_map/psum | solution.py:64
  554.6 17.5 %reduce-scatter.8.cloned.1.call-done = f32[384,2048]{1,0:T(8,128)} async-done(((f32[768,2048]{1,0:T(8,128)}), f32[384,2048]{1,0:T(8,128)}) %reduce-scatter.8.cloned.1.call-update) | async-done | bytes 3145744 | tf_op jit(solution)/shard_map/reduce_scatter | solution.py:56
  576.1 119.5 %all-reduce.5.cloned.1.call-done = f32[768,512]{1,0:T(8,128)} async-done(((f32[768,512]{1,0:T(8,128)}), f32[768,512]{1,0:T(8,128)}) %all-reduce.5.cloned.1.call-update) | async-done | bytes 1572880 | tf_op jit(solution)/shard_map/psum | solution.py:64
  (61 shorter events, 116.9 us)
Async XLA Ops:
  7.2 67.8 %all-gather.2.cloned.1.call-start = ((), (), s32[]{:S(2)}) async-start(), calls=%async_computation.3 | async-start | bytes 3932160 | tf_op jit(solution)/shard_map/all_gather | solution.py:17
  7.9 493.9 %reduce-scatter.4.cloned.1.call-start = ((), (), s32[]{:S(2)}) async-start(), calls=%async_computation.4 | async-start | bytes 5242880 | tf_op jit(solution)/shard_map/reduce_scatter | solution.py:54
  78.1 5.9 copy-start.1
  389.7 142.1 %reduce-scatter.6.cloned.1.call-start = ((), (), s32[]{:S(2)}) async-start(), calls=%async_computation.5 | async-start | bytes 1310720 | tf_op jit(solution)/shard_map/reduce_scatter | solution.py:55
  501.8 52.8 %all-reduce.3.cloned.1.call-start = ((), (), s32[]{:S(2)}) async-start(), calls=%async_computation.7 | async-start | bytes 3145728 | tf_op jit(solution)/shard_map/psum | solution.py:64
  534.7 37.3 %reduce-scatter.8.cloned.1.call-start = ((), (), s32[]{:S(2)}) async-start(), calls=%async_computation.6 | async-start | bytes 9437184 | tf_op jit(solution)/shard_map/reduce_scatter | solution.py:56
  541.2 30.9 %copy-start = (f32[384,2048]{1,0:T(8,128)S(1)}, f32[384,2048]{1,0:T(8,128)}, u32[]{:S(2)}) copy-start(f32[384,2048]{1,0:T(8,128)} %param.13) | copy-start | bytes 9437188
  541.2 154.4 %all-reduce.5.cloned.1.call-start = ((), (), s32[]{:S(2)}) async-start(), calls=%async_computation.8 | async-start | bytes 3145728 | tf_op jit(solution)/shard_map/psum | solution.py:64
Sparse Core Ops, SparseCore 0:
  9.5 65.3 all-gather.1
  389.8 111.9 reduce-scatter.3
  504.6 27.0 reduce-scatter.5
  534.9 19.6 all-reduce.2
  556.7 15.3 reduce-scatter.7
  577.3 118.2 all-reduce.4
